TPU v7x, 32 devices: a whole 2x2x4 slice. The times are simulated.
32 devices in a mesh: ctx: 16 (over z, y, core), fsdp: 2 (over x).
Axes of the slice: x: 2, y: 2, z: 4, core: 2. Of those that a mesh axis runs over, the one named last changes fastest.
Arguments:
- layer_input: bfloat16 [2, 4096, 768], P('fsdp', 'ctx'), may hold values from -6 to 6
- doc_lengths: int32 [2, 16], P('fsdp'), may hold values from 1 to 2048, 4096 in all within a row
- ln1_gain: bfloat16 [768], P('fsdp'), may hold values from 0.5 to 1.5
- ln1_bias: bfloat16 [768], P('fsdp'), may hold values from -3 to 3
- ln2_gain: bfloat16 [768], P('fsdp'), may hold values from 0.5 to 1.5
- ln2_bias: bfloat16 [768], P('fsdp'), may hold values from -3 to 3
- qkv_weight: bfloat16 [768, 896], P('fsdp'), may hold values from -0.21875 to 0.21875
- qkv_bias: bfloat16 [896], P('fsdp'), may hold values from -3 to 3
- out_weight: bfloat16 [768, 768], P('fsdp'), may hold values from -1 to 1
- out_bias: bfloat16 [768], P('fsdp'), may hold values from -3 to 3
- up_weight: bfloat16 [768, 3072], P('fsdp'), may hold values from -0.21875 to 0.21875
- up_bias: bfloat16 [3072], P('fsdp'), may hold values from -3 to 3
- down_weight: bfloat16 [3072, 768], P('fsdp'), may hold values from -0.109375 to 0.109375
- down_bias: bfloat16 [768], P('fsdp'), may hold values from -3 to 3
- out_grad: bfloat16 [2, 4096, 768], P('fsdp', 'ctx'), may hold values from -6 to 6
- kv_grad_later: float32 [2, 4096, 128], P('fsdp', 'ctx'), may hold values from -8 to 8
Outputs:
- layer_output: bfloat16 [2, 4096, 768], P('fsdp', 'ctx')
- x_grad: float32 [2, 4096, 768], P('fsdp', 'ctx')
- ln1_gain_grad: float32 [768], P('fsdp')
- ln1_bias_grad: float32 [768], P('fsdp')
- ln2_gain_grad: float32 [768], P('fsdp')
- ln2_bias_grad: float32 [768], P('fsdp')
- qkv_weight_grad: float32 [768, 896], P('fsdp')
- qkv_bias_grad: float32 [896], P('fsdp')
- out_weight_grad: float32 [768, 768], P('fsdp')
- out_bias_grad: float32 [768], P('fsdp')
- up_weight_grad: float32 [768, 3072], P('fsdp')
- up_bias_grad: float32 [3072], P('fsdp')
- down_weight_grad: float32 [3072, 768], P('fsdp')
- down_bias_grad: float32 [768], P('fsdp')
Inputs may be any that keep to these rules, and one draw needn't show every extreme that they name: `doc_lengths`: each row lists the 16 documents of one stream in order; they fill its 4096 tokens and the longest has exactly 2048.
All inputs are finite; a program needn't handle non-finite values.
Results may differ from a plain program's by a relative error of at most 0.011.
Values may be sent and summed in bfloat16 or wider, within the bound.
No kernel may reach another device: no remote copies, remote signals or barrier semaphores. Data moves between devices by JAX's collectives and lax.ppermute only.
A program may use at most 192 MiB of HBM per device.

v0:
```python
from functools import partial

import jax
import jax.numpy as jnp
from jax import lax
from jax.sharding import PartitionSpec as P

ROT = 16


def layer_parts(values, norm_gain, norm_shift):
    centred = values - jnp.mean(values, axis=-1, keepdims=True)
    inverse_root = lax.rsqrt(jnp.mean(centred * centred, axis=-1, keepdims=True) + 1e-05)
    normed = centred * inverse_root
    return (normed * norm_gain + norm_shift, normed, inverse_root)


def norm_back(grad_norm, normed, inverse_root, norm_gain):
    upstream = grad_norm * norm_gain
    return inverse_root * (
        upstream
        - jnp.mean(upstream, axis=-1, keepdims=True)
        - normed * jnp.mean(upstream * normed, axis=-1, keepdims=True)
    )


def turn_tables(positions):
    half_rot = ROT // 2
    frequencies = 10000.0 ** (-jnp.arange(half_rot, dtype=jnp.float32) / half_rot)
    angles = positions[:, None] * frequencies[None, :]
    cosine_table = jnp.concatenate([jnp.cos(angles), jnp.cos(angles)], axis=-1)[:, None, :]
    sine_table = jnp.concatenate([jnp.sin(angles), jnp.sin(angles)], axis=-1)[:, None, :]
    return (cosine_table, sine_table)


def rotate(values, cosine_table, sine_table):
    half_rot = ROT // 2
    leading = values[..., :ROT]
    turned = (
        leading * cosine_table
        + jnp.concatenate([-leading[..., half_rot:], leading[..., :half_rot]], axis=-1) * sine_table
    )
    return jnp.concatenate([turned, values[..., ROT:]], axis=-1)


def unrotate(grads, cosine_table, sine_table):
    half_rot = ROT // 2
    leading = grads[..., :ROT]
    moved = leading * sine_table
    turned = leading * cosine_table + jnp.concatenate(
        [moved[..., half_rot:], -moved[..., :half_rot]], axis=-1
    )
    return jnp.concatenate([turned, grads[..., ROT:]], axis=-1)


def to_order(gathered, devices):
    columns = gathered.shape[-1]
    halves = gathered.reshape(devices, 2, -1, columns)
    return jnp.concatenate(
        [halves[:, 0].reshape(-1, columns), halves[::-1, 1].reshape(-1, columns)], axis=0
    )


def from_order(ordered, devices):
    columns = ordered.shape[-1]
    middle = ordered.shape[0] // 2
    lower = ordered[:middle].reshape(devices, -1, columns)
    upper = ordered[middle:].reshape(devices, -1, columns)[::-1]
    return jnp.stack([lower, upper], axis=1).reshape(-1, columns)


def inner_rows(left, right):
    return lax.dot_general(
        left, right, (((0,), (0,)), ((), ())), preferred_element_type=jnp.float32
    )


def outer_cols(left, right):
    return lax.dot_general(
        left, right, (((1,), (1,)), ((), ())), preferred_element_type=jnp.float32
    )


def gelu_slope(values):
    return (
        0.5 * (1.0 + lax.erf(values * 0.7071067811865476))
        + values * jnp.exp(-0.5 * values * values) * 0.3989422804014327
    )


def masked_scores(q_part, p_part, s_part, ordered, block_index, key_block, score_scale, head_size):
    key_piece = lax.dynamic_slice_in_dim(ordered, block_index * key_block, key_block, 0)
    key_places = block_index * key_block + jnp.arange(key_block, dtype=jnp.int32)
    scores = (
        jnp.einsum(
            "thd,kd->thk", q_part, key_piece[:, :head_size], preferred_element_type=jnp.float32
        )
        * score_scale
    )
    allowed = (key_places[None, :] <= p_part[:, None]) & (key_places[None, :] >= s_part[:, None])
    return (jnp.where(allowed[:, None, :], scores, -1e30), key_piece)


def forward_step(
    block_index, state_now, q_part, p_part, s_part, ordered, key_block, score_scale, head_size
):
    row_peak, row_total, weighted = state_now
    scores, key_piece = masked_scores(
        q_part, p_part, s_part, ordered, block_index, key_block, score_scale, head_size
    )
    new_peak = jnp.maximum(row_peak, jnp.max(scores, axis=-1))
    weights = jnp.exp(scores - new_peak[..., None])
    factor = jnp.exp(row_peak - new_peak)
    row_total = row_total * factor + jnp.sum(weights, axis=-1)
    weighted = weighted * factor[..., None] + jnp.einsum(
        "thk,kd->thd",
        weights.astype(jnp.bfloat16),
        key_piece[:, head_size:],
        preferred_element_type=jnp.float32,
    )
    return (new_peak, row_total, weighted)


def backward_step(
    block_index,
    state_now,
    q_part,
    p_part,
    s_part,
    g_part,
    d_part,
    l_part,
    ordered,
    key_block,
    score_scale,
    head_size,
):
    grad_query, grad_pair = state_now
    scores, key_piece = masked_scores(
        q_part, p_part, s_part, ordered, block_index, key_block, score_scale, head_size
    )
    probabilities = jnp.exp(scores - l_part[..., None])
    grad_probs = jnp.einsum(
        "thd,kd->thk", g_part, key_piece[:, head_size:], preferred_element_type=jnp.float32
    )
    grad_scores = (probabilities * (grad_probs - d_part[..., None])).astype(jnp.bfloat16)
    grad_query = (
        grad_query
        + jnp.einsum(
            "thk,kd->thd", grad_scores, key_piece[:, :head_size], preferred_element_type=jnp.float32
        )
        * score_scale
    )
    grad_keys = (
        jnp.einsum("thk,thd->kd", grad_scores, q_part, preferred_element_type=jnp.float32)
        * score_scale
    )
    grad_values = jnp.einsum(
        "thk,thd->kd",
        probabilities.astype(jnp.bfloat16),
        g_part,
        preferred_element_type=jnp.float32,
    )
    update = lax.dynamic_slice_in_dim(
        grad_pair, block_index * key_block, key_block, 0
    ) + jnp.concatenate([grad_keys, grad_values], axis=1)
    grad_pair = lax.dynamic_update_slice_in_dim(grad_pair, update, block_index * key_block, 0)
    return (grad_query, grad_pair)


def body(
    layer_input,
    doc_lengths,
    ln1_gain,
    ln1_bias,
    ln2_gain,
    ln2_bias,
    qkv_weight,
    qkv_bias,
    out_weight,
    out_bias,
    up_weight,
    up_bias,
    down_weight,
    down_bias,
    out_grad,
    kv_grad_later,
):
    devices = lax.axis_size("ctx")
    place_index = lax.axis_index("ctx")
    tokens = layer_input.shape[1]
    half_rows = tokens // 2
    width = layer_input.shape[2]
    head_size = kv_grad_later.shape[2] // 2
    head_count = width // head_size
    score_scale = head_size ** (-0.5)
    (
        first_gain,
        first_shift,
        second_gain,
        second_shift,
        w_qkv,
        bias_qkv,
        w_out,
        bias_out,
        w_up,
        bias_up,
        w_down,
        bias_down,
    ) = (
        lax.all_gather(ln1_gain, "fsdp", axis=0, tiled=True),
        lax.all_gather(ln1_bias, "fsdp", axis=0, tiled=True),
        lax.all_gather(ln2_gain, "fsdp", axis=0, tiled=True),
        lax.all_gather(ln2_bias, "fsdp", axis=0, tiled=True),
        lax.all_gather(qkv_weight, "fsdp", axis=0, tiled=True),
        lax.all_gather(qkv_bias, "fsdp", axis=0, tiled=True),
        lax.all_gather(out_weight, "fsdp", axis=0, tiled=True),
        lax.all_gather(out_bias, "fsdp", axis=0, tiled=True),
        lax.all_gather(up_weight, "fsdp", axis=0, tiled=True),
        lax.all_gather(up_bias, "fsdp", axis=0, tiled=True),
        lax.all_gather(down_weight, "fsdp", axis=0, tiled=True),
        lax.all_gather(down_bias, "fsdp", axis=0, tiled=True),
    )
    first_gain = first_gain.astype(jnp.float32)
    second_gain = second_gain.astype(jnp.float32)
    offsets = jnp.arange(half_rows, dtype=jnp.int32)
    places = jnp.concatenate(
        [place_index * half_rows + offsets, (2 * devices - 1 - place_index) * half_rows + offsets]
    )
    lengths = doc_lengths[0]
    doc_ends = jnp.cumsum(lengths)
    starts = jnp.sum(jnp.where(doc_ends[None, :] <= places[:, None], lengths[None, :], 0), axis=1)
    inputs = layer_input[0].astype(jnp.float32)
    first_norm, first_hat, first_root = layer_parts(
        inputs, first_gain, first_shift.astype(jnp.float32)
    )
    second_norm, second_hat, second_root = layer_parts(
        inputs, second_gain, second_shift.astype(jnp.float32)
    )
    first_low = first_norm.astype(jnp.bfloat16)
    second_low = second_norm.astype(jnp.bfloat16)
    mixed_proj = jnp.dot(first_low, w_qkv, preferred_element_type=jnp.float32) + bias_qkv.astype(
        jnp.float32
    )
    cosine_table, sine_table = turn_tables(places.astype(jnp.float32))
    queries = rotate(
        mixed_proj[:, :width].reshape(tokens, head_count, head_size), cosine_table, sine_table
    ).astype(jnp.bfloat16)
    key_rows = rotate(
        mixed_proj[:, width : width + head_size].reshape(tokens, 1, head_size),
        cosine_table,
        sine_table,
    )[:, 0]
    key_values = jnp.concatenate([key_rows, mixed_proj[:, width + head_size :]], axis=1).astype(
        jnp.bfloat16
    )
    gathered = lax.all_gather(key_values, "ctx", axis=0, tiled=True)
    ordered = to_order(gathered, devices)
    stream = ordered.shape[0]
    key_block = min(2048, stream)
    attended_parts = []
    logsum_parts = []
    for side_index in range(2):
        q_part = queries[side_index * half_rows : (side_index + 1) * half_rows]
        p_part = places[side_index * half_rows : (side_index + 1) * half_rows]
        s_part = starts[side_index * half_rows : (side_index + 1) * half_rows]
        first_block = jnp.min(s_part) // key_block
        stop_block = jnp.max(p_part) // key_block + 1
        start_state = (
            jnp.full((half_rows, head_count), -1e30, jnp.float32),
            jnp.zeros((half_rows, head_count), jnp.float32),
            jnp.zeros((half_rows, head_count, head_size), jnp.float32),
        )
        step_fn = partial(
            forward_step,
            q_part=q_part,
            p_part=p_part,
            s_part=s_part,
            ordered=ordered,
            key_block=key_block,
            score_scale=score_scale,
            head_size=head_size,
        )
        row_peak, row_total, weighted = lax.fori_loop(first_block, stop_block, step_fn, start_state)
        attended_parts.append(weighted / row_total[..., None])
        logsum_parts.append(row_peak + jnp.log(row_total))
    attended = jnp.concatenate(attended_parts, axis=0)
    logsums = jnp.concatenate(logsum_parts, axis=0)
    attended_low = attended.reshape(tokens, width).astype(jnp.bfloat16)
    attention = jnp.dot(attended_low, w_out, preferred_element_type=jnp.float32) + bias_out.astype(
        jnp.float32
    )
    hidden = jnp.dot(second_low, w_up, preferred_element_type=jnp.float32) + bias_up.astype(
        jnp.float32
    )
    act_low = jax.nn.gelu(hidden, approximate=False).astype(jnp.bfloat16)
    feed_forward = jnp.dot(act_low, w_down, preferred_element_type=jnp.float32) + bias_down.astype(
        jnp.float32
    )
    result = (inputs + attention + feed_forward).astype(jnp.bfloat16)[None]
    grad_out = out_grad[0]
    grad_float = grad_out.astype(jnp.float32)
    grad_hidden = (outer_cols(grad_out, w_down) * gelu_slope(hidden)).astype(jnp.bfloat16)
    grad_second = outer_cols(grad_hidden, w_up)
    grad_attended = outer_cols(grad_out, w_out).astype(jnp.bfloat16)
    grad_heads = grad_attended.reshape(tokens, head_count, head_size)
    row_delta = jnp.sum(grad_heads.astype(jnp.float32) * attended, axis=-1)
    grad_pair = jnp.zeros((stream, 2 * head_size), jnp.float32)
    query_parts = []
    for side_index in range(2):
        q_part = queries[side_index * half_rows : (side_index + 1) * half_rows]
        p_part = places[side_index * half_rows : (side_index + 1) * half_rows]
        s_part = starts[side_index * half_rows : (side_index + 1) * half_rows]
        first_block = jnp.min(s_part) // key_block
        stop_block = jnp.max(p_part) // key_block + 1
        step_fn = partial(
            backward_step,
            q_part=q_part,
            p_part=p_part,
            s_part=s_part,
            g_part=grad_heads[side_index * half_rows : (side_index + 1) * half_rows],
            d_part=row_delta[side_index * half_rows : (side_index + 1) * half_rows],
            l_part=logsums[side_index * half_rows : (side_index + 1) * half_rows],
            ordered=ordered,
            key_block=key_block,
            score_scale=score_scale,
            head_size=head_size,
        )
        grad_query, grad_pair = lax.fori_loop(
            first_block,
            stop_block,
            step_fn,
            (jnp.zeros((half_rows, head_count, head_size), jnp.float32), grad_pair),
        )
        query_parts.append(grad_query)
    owned_pair = (
        lax.psum_scatter(from_order(grad_pair, devices), "ctx", scatter_dimension=0, tiled=True)
        + kv_grad_later[0]
    )
    grad_key_rows = unrotate(
        owned_pair[:, :head_size].reshape(tokens, 1, head_size), cosine_table, sine_table
    )[:, 0]
    grad_queries = unrotate(jnp.concatenate(query_parts, axis=0), cosine_table, sine_table).reshape(
        tokens, width
    )
    grad_mixed = jnp.concatenate(
        [grad_queries, grad_key_rows, owned_pair[:, head_size:]], axis=1
    ).astype(jnp.bfloat16)
    grad_first = outer_cols(grad_mixed, w_qkv)
    grad_inputs = (
        grad_float
        + norm_back(grad_first, first_hat, first_root, first_gain)
        + norm_back(grad_second, second_hat, second_root, second_gain)
    )
    first_gain_grad = jnp.sum(grad_first * first_hat, axis=0)
    first_shift_grad = jnp.sum(grad_first, axis=0)
    second_gain_grad = jnp.sum(grad_second * second_hat, axis=0)
    second_shift_grad = jnp.sum(grad_second, axis=0)
    bias_qkv_grad = jnp.sum(grad_mixed.astype(jnp.float32), axis=0)
    bias_out_grad = jnp.sum(grad_float, axis=0)
    bias_up_grad = jnp.sum(grad_hidden.astype(jnp.float32), axis=0)
    bias_down_grad = jnp.sum(grad_float, axis=0)
    shards = (
        lax.psum_scatter(
            first_gain_grad.astype(jnp.bfloat16), "fsdp", scatter_dimension=0, tiled=True
        ).astype(jnp.float32),
        lax.psum_scatter(
            first_shift_grad.astype(jnp.bfloat16), "fsdp", scatter_dimension=0, tiled=True
        ).astype(jnp.float32),
        lax.psum_scatter(
            second_gain_grad.astype(jnp.bfloat16), "fsdp", scatter_dimension=0, tiled=True
        ).astype(jnp.float32),
        lax.psum_scatter(
            second_shift_grad.astype(jnp.bfloat16), "fsdp", scatter_dimension=0, tiled=True
        ).astype(jnp.float32),
        lax.psum_scatter(
            inner_rows(first_low, grad_mixed).astype(jnp.bfloat16),
            "fsdp",
            scatter_dimension=0,
            tiled=True,
        ).astype(jnp.float32),
        lax.psum_scatter(
            bias_qkv_grad.astype(jnp.bfloat16), "fsdp", scatter_dimension=0, tiled=True
        ).astype(jnp.float32),
        lax.psum_scatter(
            inner_rows(attended_low, grad_out).astype(jnp.bfloat16),
            "fsdp",
            scatter_dimension=0,
            tiled=True,
        ).astype(jnp.float32),
        lax.psum_scatter(
            bias_out_grad.astype(jnp.bfloat16), "fsdp", scatter_dimension=0, tiled=True
        ).astype(jnp.float32),
        lax.psum_scatter(
            inner_rows(second_low, grad_hidden).astype(jnp.bfloat16),
            "fsdp",
            scatter_dimension=0,
            tiled=True,
        ).astype(jnp.float32),
        lax.psum_scatter(
            bias_up_grad.astype(jnp.bfloat16), "fsdp", scatter_dimension=0, tiled=True
        ).astype(jnp.float32),
        lax.psum_scatter(
            inner_rows(act_low, grad_out).astype(jnp.bfloat16),
            "fsdp",
            scatter_dimension=0,
            tiled=True,
        ).astype(jnp.float32),
        lax.psum_scatter(
            bias_down_grad.astype(jnp.bfloat16), "fsdp", scatter_dimension=0, tiled=True
        ).astype(jnp.float32),
    )
    totals = lax.psum(
        (
            shards[0],
            shards[1],
            shards[2],
            shards[3],
            shards[4],
            shards[5],
            shards[6],
            shards[7],
            shards[8],
            shards[9],
            shards[10],
            shards[11],
        ),
        "ctx",
    )
    return (
        result,
        grad_inputs[None],
        totals[0],
        totals[1],
        totals[2],
        totals[3],
        totals[4],
        totals[5],
        totals[6],
        totals[7],
        totals[8],
        totals[9],
        totals[10],
        totals[11],
    )


def solution(mesh):
    return jax.shard_map(
        body,
        mesh=mesh,
        in_specs=(
            P("fsdp", "ctx", None),
            P("fsdp", None),
            P("fsdp"),
            P("fsdp"),
            P("fsdp"),
            P("fsdp"),
            P("fsdp", None),
            P("fsdp"),
            P("fsdp", None),
            P("fsdp"),
            P("fsdp", None),
            P("fsdp"),
            P("fsdp", None),
            P("fsdp"),
            P("fsdp", "ctx", None),
            P("fsdp", "ctx", None),
        ),
        out_specs=(
            P("fsdp", "ctx", None),
            P("fsdp", "ctx", None),
            P("fsdp"),
            P("fsdp"),
            P("fsdp"),
            P("fsdp"),
            P("fsdp", None),
            P("fsdp"),
            P("fsdp", None),
            P("fsdp"),
            P("fsdp", None),
            P("fsdp"),
            P("fsdp", None),
            P("fsdp"),
        ),
        check_vma=False,
    )
```

profile of v0, /device:TPU:0, one launch (start us, length us, event | category | flops | bytes accessed | tf_op | source)
XLA Modules:
  0.0 852.8 jit_solution(14559245818193893010)
XLA Ops:
  15.3 5.8 all-reduce
  31.6 5.7 all-gather.13.cloned.1.call-done
  52.3 9.5 %all-gather.17.cloned.1.call-done = bf16[768,768]{1,0:T(8,128)(2,1)} async-done(((bf16[384,768]{1,0:T(8,128)(2,1)}), bf16[768,768]{1,0:T(8,128)(2,1)}) %all-gather.17.cloned.1.call-update) | async-done | bytes 1179664 | tf_op jit(solution)/shard_map/all_gather | solution.py:217
  66.8 35.7 %all-gather.15.cloned.1.call-done = bf16[4096,128]{1,0:T(8,128)(2,1)} async-done(((bf16[256,128]{1,0:T(8,128)(2,1)}), bf16[4096,128]{1,0:T(8,128)(2,1)}) %all-gather.15.cloned.1.call-update) | async-done | bytes 1048592 | tf_op jit(solution)/shard_map/all_gather | solution.py:257
  104.4 13.0 %while.57 = (s32[]{:T(128)}, f32[128,12]{0,1:T(8,128)S(1)}, f32[128,12]{0,1:T(8,128)S(1)}, f32[128,12,64]{0,2,1:T(8,128)S(1)}, s32[]{:T(128)}, /*index=5*/s32[12...) while((s32[]{:T(128)}, f32[128,12]{0,1:T(8,128)S(1)}, ...), condition=%wide.region_15.16_spmd.clone, body=%wide.region_12.15_spmd.clone.sunk | while | flops 840897664 | bytes 90756848 | solution.py:284
  111.2 6.2 fusion.225
  118.1 13.2 %while.56 = (s32[]{:T(128)}, f32[128,12]{0,1:T(8,128)S(1)}, f32[128,12]{0,1:T(8,128)S(1)}, f32[128,12,64]{0,2,1:T(8,128)S(1)}, s32[]{:T(128)}, /*index=5*/s32[12...) while((s32[]{:T(128)}, f32[128,12]{0,1:T(8,128)S(1)}, ...), condition=%wide.region_9.10_spmd.clone, body=%wide.region_6.9_spmd.clone.sunk | while | flops 840897664 | bytes 90756848 | solution.py:284
  125.1 6.2 fusion.220
  135.2 23.4 %while.58 = (s32[]{:T(128)}, f32[128,12,64]{0,2,1:T(8,128)}, f32[4096,128]{0,1:T(8,128)S(1)}, s32[]{:T(128)}, s32[128]{0:T(128)}, /*index=5*/bf16[4096,128]{0,1:...) while((s32[]{:T(128)}, f32[128,12,64]{0,2,1:T(8,128)}, ...), condition=%wide.region_18.19_spmd.clone, body=%wide.region_17.18_spmd.clone.sunk | while | flops 2046363776 | bytes 116193160 | solution.py:329
  135.7 6.4 fusion.233
  143.1 6.9 fusion.234
  159.4 24.3 %while.59 = (s32[]{:T(128)}, f32[128,12,64]{0,2,1:T(8,128)}, f32[4096,128]{0,1:T(8,128)S(1)}, s32[]{:T(128)}, s32[128]{0:T(128)}, /*index=5*/bf16[4096,128]{0,1:...) while((s32[]{:T(128)}, f32[128,12,64]{0,2,1:T(8,128)}, ...), condition=%wide.region_20.21_spmd.clone, body=%wide.region_19.20_spmd.clone.sunk | while | flops 2046363776 | bytes 116246464 | solution.py:329
  159.6 6.4 fusion.246
  167.0 6.9 fusion.247
  205.4 80.7 %reduce-scatter.6.cloned.1.call-done = f32[256,128]{1,0:T(8,128)} async-done(((f32[4096,128]{1,0:T(8,128)}), f32[256,128]{1,0:T(8,128)}) %reduce-scatter.6.cloned.1.call-update) | async-done | bytes 131088 | tf_op jit(solution)/shard_map/reduce_scatter | solution.py:337
  290.0 59.3 %all-gather.19.cloned.1.call-done = bf16[768,3072]{1,0:T(8,128)(2,1)} async-done(((bf16[384,3072]{1,0:T(8,128)(2,1)}), bf16[768,3072]{1,0:T(8,128)(2,1)}) %all-gather.19.cloned.1.call-update) | async-done | bytes 4718608 | tf_op jit(solution)/shard_map/all_gather | solution.py:219
  349.3 10.8 %fusion.73 = (bf16[256,3072]{1,0:T(8,128)(2,1)S(1)}, f32[256,3072]{1,0:T(8,128)}) fusion(f32[3072]{0:T(1024)S(1)} %bitcast.345, bf16[768,3072]{1,0:T(8,128)(2,1)} %all-gather.19.cloned.1.call-done, bf16[1,256,768]{2,1,0:T(8,128)(2,1)S(1)} %copy-done.8, f32[768]{0:T(1024)S(1)} %reshape.480, f32[768]{0:T(1024)S(1)} %reshape.479, f32[256]{0:T(256)S(1)} %copy-done.50, ...), kind=kOutput, calls=%fused_computation.101 | convolution fusion | flops 1261043712 | bytes 9850880 | tf_op jit(solution)/shard_map/dot_general | solution.py:293
  360.1 53.4 %all-gather.21.cloned.1.call-done = bf16[3072,768]{1,0:T(8,128)(2,1)} async-done(((bf16[1536,768]{1,0:T(8,128)(2,1)}), bf16[3072,768]{1,0:T(8,128)(2,1)}) %all-gather.21.cloned.1.call-update) | async-done | bytes 4718608 | tf_op jit(solution)/shard_map/all_gather | solution.py:221
  413.4 6.9 fusion.151
  448.8 4.6 fusion.152
  456.4 7.9 all-reduce.9
  466.2 62.1 %reduce-scatter.12.cloned.1.call-done = bf16[384,3072]{1,0:T(8,128)(2,1)} async-done(((bf16[768,3072]{1,0:T(8,128)(2,1)}), bf16[384,3072]{1,0:T(8,128)(2,1)}) %reduce-scatter.12.cloned.1.call-update) | async-done | bytes 2359312 | tf_op jit(solution)/shard_map/reduce_scatter | solution.py:394
  528.4 62.8 %reduce-scatter.14.cloned.1.call-done = bf16[1536,768]{1,0:T(8,128)(2,1)} async-done(((bf16[3072,768]{1,0:T(8,128)(2,1)}), bf16[1536,768]{1,0:T(8,128)(2,1)}) %reduce-scatter.14.cloned.1.call-update) | async-done | bytes 2359312 | tf_op jit(solution)/shard_map/reduce_scatter | solution.py:403
  591.1 253.8 %all-reduce.11 = (f32[384]{0:T(512)}, f32[384]{0:T(512)}, f32[384]{0:T(512)}, f32[384]{0:T(512)}, f32[384,896]{1,0:T(8,128)}, /*index=5*/f32[448]{0:T(512)}, f32...) all-reduce(f32[384]{0:T(512)S(1)} %dynamic-slice_convert_fusion.6, ...), channel_id=1, replica_groups=mesh['ctx'=16,'fsdp'=2] {'ctx'}, use_global_device_ids=true, to_apply=%region_28.29 | all-reduce | flops 3002176 | bytes 18020864 | tf_op jit(solution)/shard_map/psum | solution.py:413
  (319 shorter events, 125.4 us)
Async XLA Ops:
  7.2 30.2 %all-gather.13.cloned.1.call-start = ((), (), s32[]{:S(2)}) async-start(), calls=%async_computation.5 | async-start | bytes 2064384 | tf_op jit(solution)/shard_map/all_gather | solution.py:215
  7.9 53.8 %all-gather.17.cloned.1.call-start = ((), (), s32[]{:S(2)}) async-start(), calls=%async_computation.7 | async-start | bytes 1769472 | tf_op jit(solution)/shard_map/all_gather | solution.py:217
  8.7 93.8 %all-gather.15.cloned.1.call-start = ((), (), s32[]{:S(2)}) async-start(), calls=%async_computation.6 | async-start | bytes 1114112 | tf_op jit(solution)/shard_map/all_gather | solution.py:257
  9.9 30.9 %copy-start.63 = (s32[1,16]{1,0:T(1,128)S(1)}, s32[1,16]{1,0:T(1,128)}, u32[]{:S(2)}) copy-start(s32[1,16]{1,0:T(1,128)} %param.25) | copy-start | bytes 196
  11.1 50.6 %copy-start.9 = (bf16[1,256,768]{2,1,0:T(8,128)(2,1)S(1)}, bf16[1,256,768]{2,1,0:T(8,128)(2,1)}, u32[]{:S(2)}) copy-start(bf16[1,256,768]{2,1,0:T(8,128)(2,1)} %param.38) | copy-start | bytes 1179652
  31.5 35.1 %copy-start.29 = (f32[256,16]{0,1:T(8,128)}, f32[256,16]{0,1:T(8,128)S(1)}, u32[]{:S(2)}) copy-start(f32[256,16]{0,1:T(8,128)S(1)} %pad_maximum_fusion.7) | copy-start | bytes 49156
  40.8 245.3 %reduce-scatter.6.cloned.1.call-start = ((), (), s32[]{:S(2)}) async-start(), calls=%async_computation.10 | async-start | bytes 2228224 | tf_op jit(solution)/shard_map/reduce_scatter | solution.py:337
  188.4 160.8 %all-gather.19.cloned.1.call-start = ((), (), s32[]{:S(2)}) async-start(), calls=%async_computation.8 | async-start | bytes 7077888 | tf_op jit(solution)/shard_map/all_gather | solution.py:219
  189.0 224.4 %all-gather.21.cloned.1.call-start = ((), (), s32[]{:S(2)}) async-start(), calls=%async_computation.9 | async-start | bytes 7077888 | tf_op jit(solution)/shard_map/all_gather | solution.py:221
  189.6 263.8 %reduce-scatter.10.cloned.1.call-start = ((), (), s32[]{:S(2)}) async-start(), calls=%async_computation.12 | async-start | bytes 1769472 | tf_op jit(solution)/shard_map/reduce_scatter | solution.py:385
  203.6 82.5 %copy-start.39 = (f32[1,256,128]{2,1,0:T(8,128)S(1)}, f32[1,256,128]{2,1,0:T(8,128)}, u32[]{:S(2)}) copy-start(f32[1,256,128]{2,1,0:T(8,128)} %param.39) | copy-start | bytes 393220
  203.7 83.8 %copy-start.24 = (f32[256,16]{1,0:T(8,128)S(1)}, f32[256,16]{1,0:T(8,128)}, u32[]{:S(2)}) copy-start(f32[256,16]{1,0:T(8,128)} %copy-done.23) | copy-start | bytes 49156
  205.2 82.6 %copy-start.8 = (bf16[1,256,768]{2,1,0:T(8,128)(2,1)S(1)}, bf16[1,256,768]{2,1,0:T(8,128)(2,1)}, u32[]{:S(2)}) copy-start(bf16[1,256,768]{2,1,0:T(8,128)(2,1)} %param.24) | copy-start | bytes 1179652
  205.2 82.6 %copy-start.45 = (f32[256]{0:T(256)S(1)}, f32[256]{0:T(256)}, u32[]{:S(2)}) copy-start(f32[256]{0:T(256)} %copy-done.44) | copy-start | bytes 3076
  205.2 82.6 %copy-start.47 = (f32[768]{0:T(1024)S(1)}, f32[768]{0:T(1024)}, u32[]{:S(2)}) copy-start(f32[768]{0:T(1024)} %copy-done.46) | copy-start | bytes 9220
  205.2 82.6 %copy-start.49 = (f32[256]{0:T(256)S(1)}, f32[256]{0:T(256)}, u32[]{:S(2)}) copy-start(f32[256]{0:T(256)} %copy-done.48) | copy-start | bytes 3076
  205.2 82.6 %copy-start.60 = (f32[768]{0:T(1024)S(1)}, f32[768]{0:T(1024)}, u32[]{:S(2)}) copy-start(f32[768]{0:T(1024)} %copy-done.59) | copy-start | bytes 9220
  205.2 261.0 %reduce-scatter.8.cloned.1.call-start = ((), (), s32[]{:S(2)}) async-start(), calls=%async_computation.11 | async-start | bytes 2064384 | tf_op jit(solution)/shard_map/reduce_scatter | solution.py:376
  287.3 62.0 %copy-start.50 = (f32[256]{0:T(256)S(1)}, f32[256]{0:T(256)}, u32[]{:S(2)}) copy-start(f32[256]{0:T(256)} %copy-done.48) | copy-start | bytes 3076
  287.3 61.9 %copy-start.52 = (f32[2,1,1536]{2,1,0:T(1,128)S(1)}, f32[2,1,1536]{2,1,0:T(1,128)}, u32[]{:S(2)}) copy-start(f32[2,1,1536]{2,1,0:T(1,128)} %convert_element_type.204) | copy-start | bytes 36868
  287.8 72.3 %copy-start.37 = (bf16[256,64]{0,1:T(8,128)(2,1)}, bf16[256,64]{0,1:T(8,128)(2,1)S(1)}, u32[]{:S(2)}) copy-start(bf16[256,64]{0,1:T(8,128)(2,1)S(1)} %copy.123) | copy-start | bytes 98308
  289.7 238.7 %reduce-scatter.12.cloned.1.call-start = ((), (), s32[]{:S(2)}) async-start(), calls=%async_computation.13 | async-start | bytes 7077888 | tf_op jit(solution)/shard_map/reduce_scatter | solution.py:394
  425.2 165.9 %reduce-scatter.14.cloned.1.call-start = ((), (), s32[]{:S(2)}) async-start(), calls=%async_computation.14 | async-start | bytes 7077888 | tf_op jit(solution)/shard_map/reduce_scatter | solution.py:403
  456.4 134.8 %copy-start.28 = (bf16[384,768]{1,0:T(8,128)(2,1)S(1)}, bf16[384,768]{1,0:T(8,128)(2,1)}, u32[]{:S(2)}) copy-start(bf16[384,768]{1,0:T(8,128)(2,1)} %reduce-scatter.10.cloned.1.call-done) | copy-start | bytes 1769476
  (52 other events, 443.8 us)
Sparse Core Ops, SparseCore 0:
  9.6 27.7 all-gather.12
  38.9 22.8 all-gather.16
  64.5 37.9 all-gather.14
  188.5 97.5 reduce-scatter.5
  287.5 61.6 all-gather.18
  350.7 62.6 all-gather.20
  416.3 21.7 reduce-scatter.9
  441.0 24.2 reduce-scatter.7
  468.3 60.0 reduce-scatter.11
  531.1 59.9 reduce-scatter.13
where the time goes:
time: 865 us; the launch traced here: 853 us
  waiting for transfers between devices  372 us (43%)
  blocking collectives  298 us (34%)
  matrix products  105 us (12%)
  between operations  28.4 us (3%)
  local copies, waits for them, and re-layouts  24.8 us (3%)
  other arithmetic  23.4 us (3%)
    psum x1, blocking collectives, body(): lax.psum((shards[0], shards[1], shards[2], shards[3], shards[4], shards[5...  254 us
    reduce_scatter x1, waiting for transfers between devices, body(): lax.psum_scatter(from_order(grad_pair, devices), 'ctx', scatter_dimension...  80.7 us
    reduce_scatter x1, waiting for transfers between devices, body(): lax.psum_scatter(inner_rows(act_low, grad_out).astype(jnp.bfloat16), 'fsd...  62.8 us
    reduce_scatter x1, waiting for transfers between devices, body(): lax.psum_scatter(inner_rows(second_low, grad_hidden).astype(jnp.bfloat16)...  62.1 us
    all_gather x1, waiting for transfers between devices, body(): lax.all_gather(up_weight, 'fsdp', axis=0, tiled=True)  59.3 us
    all_gather x1, waiting for transfers between devices, body(): lax.all_gather(down_weight, 'fsdp', axis=0, tiled=True)  53.4 us
    all_gather x1, waiting for transfers between devices, body(): gathered = lax.all_gather(key_values, 'ctx', axis=0, tiled=True)  35.7 us
  transfers between devices with their start and end apart: 10, of which 8 were waited for; matrix products, arithmetic and copies ran while one was open for 8% of the time, Pallas kernels for 0%

commit v1 on v0

v1 whole, which is shorter than its diff:
```python
from functools import partial

import jax
import jax.numpy as jnp
import numpy as np
from jax import lax
from jax.experimental import pallas as pl
from jax.experimental.pallas import tpu as pltpu
from jax.sharding import PartitionSpec as P

ROT = 16
BLOCK = 128
NT = (((1,), (1,)), ((), ()))
NN = (((1,), (0,)), ((), ()))
TN = (((0,), (0,)), ((), ()))
bf16 = jnp.bfloat16
f32 = jnp.float32


def mm(left, right, dims=NN):
    return lax.dot_general(left, right, dims, preferred_element_type=f32)


def vmem():
    return pl.BlockSpec(memory_space=pltpu.VMEM)


def smem():
    return pl.BlockSpec(memory_space=pltpu.SMEM)


def bit_reverse(index, count):
    out, left = index * 0, count
    while left > 1:
        out = out * 2 + index % 2
        index = index // 2
        left //= 2
    return out


def swap_x(value):
    return lax.ppermute(value, "fsdp", [(0, 1), (1, 0)])


def swap_ctx(value, stride, devices):
    return lax.ppermute(value, "ctx", [(i, i ^ stride) for i in range(devices)])


def in_order(bit, mine, theirs, axis=0):
    return jnp.where(
        bit == 0,
        jnp.concatenate([mine, theirs], axis=axis),
        jnp.concatenate([theirs, mine], axis=axis),
    )


def gather_bits(value, strides, devices):
    me = lax.axis_index("ctx")
    for stride in strides:
        value = in_order((me // stride) % 2, value, swap_ctx(value, stride, devices))
    return value


def scatter_bits(value, strides, devices):
    me = lax.axis_index("ctx")
    for stride in strides:
        bit = (me // stride) % 2
        half = value.shape[0] // 2
        keep = lax.dynamic_slice_in_dim(value, bit * half, half, 0)
        send = lax.dynamic_slice_in_dim(value, (1 - bit) * half, half, 0)
        value = keep.astype(f32) + swap_ctx(send.astype(bf16), stride, devices).astype(f32)
    return value


def up_strides(devices):
    out, stride = [], 1
    while stride < devices:
        out.append(stride)
        stride *= 2
    return out


def attn_kernel(
    n_dev, docs, ids_ref, len_ref, q_ref, kv_ref, g_ref, cos_ref, sin_ref,
    o_ref, dm_ref, dkv_ref, qz, gz, ot, dqt, st, bias, ds_sc, p_sc, acc,
):
    b = BLOCK
    kb = 2 * b
    width = q_ref.shape[1]
    pairs = width // 128
    me = ids_ref[0]
    low = lax.broadcasted_iota(jnp.int32, (b, 128), 1) < 64
    acc[...] = jnp.zeros_like(acc)

    def row_of(j):
        j = jnp.maximum(j, 0)
        dev = jnp.where(j < n_dev, j, 2 * n_dev - 1 - j)
        return (bit_reverse(dev, n_dev) * 2 + jnp.where(j < n_dev, 0, 1)) * b

    def half_turn(two):
        return pltpu.roll(two.astype(f32), 64, 1).astype(bf16)

    def side_step(side, carry):
        block = jnp.where(side == 0, me, 2 * n_dev - 1 - me)
        base = block * b
        rows = pl.ds(pl.multiple_of(side * b, b), b)
        qpos = base + lax.broadcasted_iota(jnp.int32, (1, b), 1)
        total = jnp.int32(0)
        qstart = jnp.zeros((1, b), jnp.int32)
        first = jnp.int32(0)
        for e in range(docs):
            size = len_ref[0, e]
            total = total + size
            qstart = qstart + jnp.where(total <= qpos, size, 0)
            first = first + jnp.where(total <= base, size, 0)
        steps = (base + b - first + kb - 1) // kb
        for p in range(pairs):
            cols = pl.ds(p * 128, 128)
            two = q_ref[rows, cols]
            zero = jnp.zeros_like(two)
            qz[pl.ds(p * 256, 128), :] = jnp.where(low, two, zero)
            qz[pl.ds(p * 256 + 128, 128), :] = jnp.where(low, half_turn(two), zero)
            two = g_ref[rows, cols]
            gz[pl.ds(p * 256, 128), :] = jnp.where(low, zero, half_turn(two))
            gz[pl.ds(p * 256 + 128, 128), :] = jnp.where(low, zero, two)
        ot[...] = jnp.zeros_like(ot)
        dqt[...] = jnp.zeros_like(dqt)
        st[0] = jnp.full(st.shape[1:], -1e30, f32)
        st[1] = jnp.zeros(st.shape[1:], f32)

        def load(t):
            hi = block - 2 * t
            r1 = pl.multiple_of(row_of(hi), b)
            r0 = pl.multiple_of(row_of(hi - 1), b)
            kvb = jnp.concatenate([kv_ref[pl.ds(r0, b), :], kv_ref[pl.ds(r1, b), :]], axis=0)
            kpos = (hi - 1) * b + lax.broadcasted_iota(jnp.int32, (kb, b), 0)
            ok = (kpos <= qpos) & (kpos >= qstart)
            bias[...] = jnp.where(ok, 0.0, -1e30)
            return kvb, r0, r1

        def forward(t, carry):
            kvb, _, _ = load(t)
            vt = kvb.astype(f32).T.astype(bf16)[64:]
            mask = bias[...]
            for p in range(pairs):
                s2 = mm(kvb, qz[pl.ds(p * 256, 256), :], NT)
                for i in range(2):
                    h = 2 * p + i
                    s = s2[:, i * 128 : (i + 1) * 128] + mask
                    old = st[0, h : h + 1, :]
                    new = jnp.maximum(old, jnp.max(s, axis=0, keepdims=True))
                    e = jnp.exp(s - new)
                    alpha = jnp.exp(old - new)
                    st[0, h : h + 1, :] = new
                    st[1, h : h + 1, :] = st[1, h : h + 1, :] * alpha + jnp.sum(e, axis=0, keepdims=True)
                    hs = pl.ds(h * 64, 64)
                    ot[hs, :] = ot[hs, :] * alpha + mm(vt, e.astype(bf16))
            return 0

        lax.fori_loop(0, steps, forward, 0)

        for p in range(pairs):
            cols = pl.ds(p * 128, 128)
            gt = g_ref[rows, cols].astype(f32).T
            halves = []
            for i in range(2):
                h = 2 * p + i
                l = st[1, h : h + 1, :]
                o = ot[pl.ds(h * 64, 64), :] / l
                halves.append(o)
                st[2, h : h + 1, :] = jnp.sum(o * gt[i * 64 : (i + 1) * 64], axis=0, keepdims=True)
                st[0, h : h + 1, :] = st[0, h : h + 1, :] + jnp.log(l)
            o_ref[rows, cols] = jnp.concatenate(halves, axis=0).T.astype(bf16)

        def backward(t, carry):
            kvb, r0, r1 = load(t)
            kt = kvb.astype(f32).T.astype(bf16)[:64]
            mask = bias[...]
            for p in range(pairs):
                s2 = mm(kvb, qz[pl.ds(p * 256, 256), :], NT)
                dp2 = mm(kvb, gz[pl.ds(p * 256, 256), :], NT)
                for i in range(2):
                    h = 2 * p + i
                    sl = slice(i * 128, (i + 1) * 128)
                    pr = jnp.exp((s2[:, sl] + mask) - st[0, h : h + 1, :])
                    ds = pr * (dp2[:, sl] - st[2, h : h + 1, :])
                    ds_sc[:, h * 128 : (h + 1) * 128] = ds.astype(bf16)
                    p_sc[:, h * 128 : (h + 1) * 128] = pr.astype(bf16)
            part = mm(ds_sc[...], qz[...]) + mm(p_sc[...], gz[...])
            acc[pl.ds(r0, b), :] += part[:b]
            acc[pl.ds(r1, b), :] += part[b:]
            dqt[...] += mm(kt, ds_sc[...])
            return 0

        lax.fori_loop(0, steps, backward, 0)

        cos = cos_ref[side]
        sin = sin_ref[side]
        for p in range(pairs):
            halves = []
            for i in range(2):
                h = 2 * p + i
                g = dqt[:, h * 128 : (h + 1) * 128] * 0.125
                g0, g1 = g[:8], g[8:16]
                halves += [g0 * cos + g1 * sin, g1 * cos - g0 * sin, g[16:]]
            dm_ref[rows, pl.ds(p * 128, 128)] = jnp.concatenate(halves, axis=0).T.astype(bf16)
        return 0

    lax.fori_loop(0, 2, side_step, 0)
    dkv_ref[...] = acc[...].astype(dkv_ref.dtype)


def attention(n_dev, me, lengths, q, kv, g, cos, sin):
    tokens, width = q.shape
    stream = kv.shape[0]
    rows = width // 64 * 128
    return pl.pallas_call(
        partial(attn_kernel, n_dev, lengths.shape[1]),
        out_shape=(
            jax.ShapeDtypeStruct((tokens, width), bf16),
            jax.ShapeDtypeStruct((tokens, width), bf16),
            jax.ShapeDtypeStruct((stream, 128), bf16),
        ),
        in_specs=[smem(), smem(), vmem(), vmem(), vmem(), vmem(), vmem()],
        out_specs=(vmem(), vmem(), vmem()),
        scratch_shapes=[
            pltpu.VMEM((rows, 128), bf16),
            pltpu.VMEM((rows, 128), bf16),
            pltpu.VMEM((width, 128), f32),
            pltpu.VMEM((64, rows), f32),
            pltpu.VMEM((3, 16, 128), f32),
            pltpu.VMEM((256, 128), f32),
            pltpu.VMEM((256, rows), bf16),
            pltpu.VMEM((256, rows), bf16),
            pltpu.VMEM((stream, 128), f32),
        ],
        cost_estimate=pl.CostEstimate(flops=20_000_000_000, transcendentals=10_000_000, bytes_accessed=4_000_000),
        name="attn",
    )(me, lengths, q, kv, g, cos, sin)


def project_kernel(scale, a_ref, w_ref, b_ref, c_ref, s1_ref, s2_ref, o_ref):
    for p in range(o_ref.shape[1] // 128):
        cols = pl.ds(p * 128, 128)
        m = mm(a_ref[...], w_ref[:, cols]) + b_ref[:, cols]
        turned = (
            m * c_ref[...]
            + pltpu.roll(m, 120, 1) * s1_ref[...]
            + pltpu.roll(m, 8, 1) * s2_ref[...]
        )
        low = turned.astype(bf16)
        o_ref[:, cols] = low if scale == 1.0 else (low.astype(f32) * scale).astype(bf16)


def project(a, w, bias, tables, scale, name):
    return pl.pallas_call(
        partial(project_kernel, scale),
        out_shape=jax.ShapeDtypeStruct((a.shape[0], w.shape[1]), bf16),
        in_specs=[vmem()] * 6,
        out_specs=vmem(),
        name=name,
    )(a, w, bias, *tables)


def layer_stats(values):
    centred = values - jnp.mean(values, axis=-1, keepdims=True)
    root = lax.rsqrt(jnp.mean(centred * centred, axis=-1, keepdims=True) + 1e-05)
    return centred * root, root


def norm_back(grad_norm, normed, root, gain):
    upstream = grad_norm * gain
    return root * (
        upstream
        - jnp.mean(upstream, axis=-1, keepdims=True)
        - normed * jnp.mean(upstream * normed, axis=-1, keepdims=True)
    )


def gelu_parts(values):
    phi = 0.5 * (1.0 + lax.erf(values * 0.7071067811865476))
    slope = phi + values * jnp.exp(-0.5 * values * values) * 0.3989422804014327
    return values * phi, slope


def body(
    layer_input, doc_lengths, ln1_gain, ln1_bias, ln2_gain, ln2_bias, qkv_weight, qkv_bias,
    out_weight, out_bias, up_weight, up_bias, down_weight, down_bias, out_grad, kv_grad_later,
):
    devices = lax.axis_size("ctx")
    me = lax.axis_index("ctx")
    side = lax.axis_index("fsdp")
    tokens, width = layer_input.shape[1:]
    half_rows = tokens // 2
    half = width // 2
    head = kv_grad_later.shape[2] // 2
    wide = up_weight.shape[1] // 2
    strides = up_strides(devices)
    near = strides[:2]

    def other_half(value, axis, size):
        return lax.dynamic_slice_in_dim(value, (1 - side) * size, size, axis)

    def own_half(value, axis, size):
        return lax.dynamic_slice_in_dim(value, side * size, size, axis)

    def fetch(value):
        part = value.shape[0] // 4
        piece = bit_reverse(me % 4, 4) * part
        return gather_bits(swap_x(lax.dynamic_slice_in_dim(value, piece, part, 0)), near[::-1], devices)

    vectors = (ln1_gain, ln1_bias, ln2_gain, ln2_bias, qkv_bias, out_bias, up_bias, down_bias)
    packed = jnp.concatenate(vectors)
    packed = jnp.pad(packed, (0, -packed.shape[0] % 1024)).reshape(-1, 128)
    packed_other = swap_x(packed).reshape(-1)
    full, at = [], 0
    for vec in vectors:
        size = vec.shape[0]
        full.append(in_order(side, vec, packed_other[at : at + size]).astype(f32)[None])
        at += size
    gain1, shift1, gain2, shift2, bias_qkv, bias_out, bias_up, bias_down = full

    w_kv = in_order(side, qkv_weight[:, width:], swap_x(qkv_weight[:, width:]))
    x_own = layer_input[0]
    x_other = swap_x(x_own)
    dy_own = out_grad[0]
    dy_other = swap_x(dy_own)
    up_other = fetch(other_half(up_weight, 1, wide))
    w_up = in_order(side, own_half(up_weight, 1, wide), up_other)
    w_q = in_order(side, qkv_weight[:, :width], fetch(qkv_weight[:, :width]))

    offsets = jnp.arange(half_rows, dtype=jnp.int32)
    places = jnp.concatenate([me * half_rows + offsets, (2 * devices - 1 - me) * half_rows + offsets]).astype(f32)
    half_rot = ROT // 2
    freq = 10000.0 ** (-jnp.arange(half_rot, dtype=f32) / half_rot)
    lane = np.arange(128)
    lane_freq = jnp.tile(freq, 128 // half_rot)[None, :]
    angles = places[:, None] * lane_freq
    cosine, sine = jnp.cos(angles), jnp.sin(angles)
    q_tables = (
        jnp.where(lane % 64 < 16, cosine, 1.0),
        jnp.where(lane % 64 < 8, -sine, 0.0),
        jnp.where((lane % 64 >= 8) & (lane % 64 < 16), sine, 0.0),
    )
    kv_tables = tuple(jnp.where(lane < 64, t, v) for t, v in zip(q_tables, (1.0, 0.0, 0.0)))
    t_angles = places.reshape(2, 1, half_rows) * freq[None, :, None]
    cos_t, sin_t = jnp.cos(t_angles), jnp.sin(t_angles)

    own_float = x_own.astype(f32)
    hat, root = layer_stats(own_float)
    hat_other, _ = layer_stats(x_other.astype(f32))
    first_own = (hat * gain1 + shift1).astype(bf16)
    first_other = (hat_other * gain1 + shift1).astype(bf16)
    second = jnp.concatenate([hat * gain2 + shift2, hat_other * gain2 + shift2], axis=0).astype(bf16)
    dy = jnp.concatenate([dy_own, dy_other], axis=0)

    kv = project(first_own, w_kv, bias_qkv[:, width:], kv_tables, 1.0, "kv")
    kv_all = gather_bits(kv, strides[::-1], devices)
    q = project(first_own, w_q, bias_qkv[:, :width], q_tables, 0.125, "q")

    d_o = mm(dy, out_weight, NT).astype(bf16)
    d_o_full = in_order(side, d_o[:tokens], swap_x(d_o[tokens:]), axis=1)

    hidden = mm(second, w_up) + own_half(bias_up, 1, wide)
    act, slope = gelu_parts(hidden)
    act = act.astype(bf16)
    d_hidden = (mm(dy, down_weight, NT) * slope).astype(bf16)
    ff = mm(act, down_weight)
    d_second = mm(d_hidden, w_up, NT)
    g_down = mm(act, dy, TN).astype(bf16)
    g_up = mm(second, d_hidden, TN).astype(bf16)
    g_up_bias = jnp.sum(d_hidden.astype(f32), axis=0)
    d_second_own = d_second[:tokens] + swap_x(d_second[tokens:].astype(bf16)).astype(f32)

    g_down_part = lax.psum_scatter(g_down, "ctx", scatter_dimension=0, tiled=True)
    g_up_part = lax.psum_scatter(g_up.reshape(2, half, wide), "ctx", scatter_dimension=1, tiled=True)
    mine = lax.dynamic_index_in_dim(g_up_part, side, 0, keepdims=False)
    theirs = swap_x(lax.dynamic_index_in_dim(g_up_part, 1 - side, 0, keepdims=False))
    g_up_part = in_order(side, mine, theirs, axis=1)
    g_down_all = lax.all_gather(g_down_part, "ctx", axis=0, tiled=True).astype(f32)
    g_up_all = lax.all_gather(g_up_part, "ctx", axis=0, tiled=True).astype(f32)

    attended, dm_q, d_kv = attention(
        devices, me.reshape(1).astype(jnp.int32), doc_lengths, q, kv_all, d_o_full, cos_t, sin_t
    )
    kv_part = scatter_bits(d_kv, strides, devices) + kv_grad_later[0]
    dk = kv_part[:, :head]
    cos_k, sin_k = cosine[:, :half_rot], sine[:, :half_rot]
    dk0, dk1 = dk[:, :half_rot], dk[:, half_rot:ROT]
    dm_kv = jnp.concatenate(
        [dk0 * cos_k + dk1 * sin_k, dk1 * cos_k - dk0 * sin_k, kv_part[:, ROT:]], axis=1
    ).astype(bf16)

    attended_other = swap_x(other_half(attended, 1, half))
    attended_half = jnp.concatenate([own_half(attended, 1, half), attended_other], axis=0)
    mixed = ff + mm(attended_half, out_weight)
    summed = mixed[:tokens] + swap_x(mixed[tokens:].astype(bf16)).astype(f32)
    result = (own_float + summed + bias_out + bias_down).astype(bf16)

    first_half = jnp.concatenate([own_half(first_own, 1, half), own_half(first_other, 1, half)], axis=0)
    dm_q_all = jnp.concatenate([dm_q, swap_x(dm_q)], axis=0)
    g_out = mm(attended_half, dy, TN)
    g_q = mm(first_half, dm_q_all, TN)
    pair = jnp.concatenate([g_q, g_out], axis=1)
    pair_part = scatter_bits(pair, strides, devices).astype(bf16)
    pair_all = gather_bits(pair_part, strides[::-1], devices).astype(f32)

    dm_kv_all = jnp.concatenate([dm_kv, swap_x(dm_kv)], axis=0)
    g_kv = mm(first_half, dm_kv_all, TN)

    d_first = mm(dm_q, w_q, NT) + mm(dm_kv, w_kv, NT)
    grad_inputs = dy_own.astype(f32) + norm_back(d_first, hat, root, gain1) + norm_back(d_second_own, hat, root, gain2)
    norms = jnp.stack(
        [
            jnp.sum(d_first * hat, axis=0),
            jnp.sum(d_first, axis=0),
            jnp.sum(d_second_own * hat, axis=0),
            jnp.sum(d_second_own, axis=0),
        ]
    )
    norms = own_half(norms, 1, half) + swap_x(other_half(norms, 1, half))
    g_dy = jnp.sum(own_half(dy, 1, half).astype(f32), axis=0)
    g_qkv_bias = jnp.concatenate(
        [jnp.sum(dm_q_all.astype(f32), axis=0), jnp.sum(dm_kv_all.astype(f32), axis=0)]
    )
    g_qkv_bias = own_half(g_qkv_bias, 0, g_qkv_bias.shape[0] // 2)
    small = jnp.concatenate([norms.reshape(-1), g_dy, g_qkv_bias, g_up_bias])
    count = small.shape[0]
    small = jnp.pad(small, (0, -count % 1024)).reshape(-1, 128)
    tail = jnp.concatenate([g_kv, small], axis=0)
    for stride in strides:
        tail = tail + swap_ctx(tail, stride, devices)
    g_kv = tail[:half]
    small = tail[half:].reshape(-1)
    norm_grads = [small[i * half : (i + 1) * half] for i in range(4)]
    at = 4 * half
    g_dy = small[at : at + half]
    at += half
    g_qkv_bias = small[at : at + qkv_bias.shape[0]]
    at += qkv_bias.shape[0]
    g_up_bias = small[at : at + wide]
    g_qkv = jnp.concatenate([pair_all[:, :width], g_kv], axis=1)
    return (
        result[None],
        grad_inputs[None],
        *norm_grads,
        g_qkv,
        g_qkv_bias,
        pair_all[:, width:],
        g_dy,
        g_up_all,
        g_up_bias,
        g_down_all,
        g_dy,
    )


def solution(mesh):
    token = P("fsdp", "ctx", None)
    vec = P("fsdp")
    mat = P("fsdp", None)
    return jax.shard_map(
        body,
        mesh=mesh,
        in_specs=(token, mat, vec, vec, vec, vec, mat, vec, mat, vec, mat, vec, mat, vec, token, token),
        out_specs=(token, token, vec, vec, vec, vec, mat, vec, mat, vec, mat, vec, mat, vec),
        check_vma=False,
    )
```

time: 865 us -> 331 us (0.38); the launches traced: 853 us -> 329 us
  blocking collectives: 298 us -> 0 us
  waiting for transfers between devices: 372 us -> 119 us
  matrix products: 105 us -> 27 us
  starting transfers between devices: 0.61 us -> 67.9 us
  other arithmetic: 23.4 us -> 45.6 us
  local copies, waits for them, and re-layouts: 24.8 us -> 39.7 us
  Pallas kernels: 0 us -> 14.3 us
  between operations: 28.4 us -> 15.1 us
    psum x1 -> x0, blocking collectives: 254 us -> none  [body(): lax.psum((shards[0], shards[1], shards[2], shards[3], shards[4], shards[5...]
    reduce_scatter x5 -> x1, waiting for transfers between devices: 206 us -> 0.01 us  [body(): lax.psum_scatter(g_down, 'ctx', scatter_dimension=0, tiled=True)]
    all_gather x5 -> x2, waiting for transfers between devices: 164 us -> 29.1 us  [the longest x1 29.1 us: body(): g_up_all = lax.all_gather(g_up_part, 'ctx', axis=0, tiled=True).astype(f32)]
    dot_general x26 -> x13, matrix products: 105 us -> 27 us  [mm(): return lax.dot_general(left, right, dims, preferred_element_type=f32)]
    ppermute x0 -> x38, waiting for transfers between devices: none -> 73.4 us  [the longest x24 55.7 us: swap_ctx(): return lax.ppermute(value, 'ctx', [(i, i ^ stride) for i in range(devices)])]
    ppermute x0 -> x38, starting transfers between devices: none -> 67.3 us  [the longest x24 51.6 us: swap_ctx(): return lax.ppermute(value, 'ctx', [(i, i ^ stride) for i in range(devices)])]
    all_gather x7 -> x0, blocking collectives: 30.6 us -> none  [the longest x1 4.57 us: body(): lax.all_gather(out_bias, 'fsdp', axis=0, tiled=True)]
    pallas_call x0 -> x3, Pallas kernels: none -> 14.3 us  [the longest x1 9.02 us: attention(): pl.pallas_call(partial(attn_kernel, n_dev, lengths.shape[1]), out_shape=(...]
  transfers between devices with their start and end apart: 10 -> 42, of which waited for: 8 -> 19; matrix products, arithmetic and copies ran while one was open for 8% -> 29% of each run, Pallas kernels for 0% -> 4%
where the time goes in v1:
time: 331 us; the launch traced here: 329 us
  waiting for transfers between devices  119 us (36%)
  starting transfers between devices  67.9 us (21%)
  other arithmetic  45.6 us (14%)
  local copies, waits for them, and re-layouts  39.7 us (12%)
  matrix products  27 us (8%)
  between operations  15.1 us (5%)
  Pallas kernels  14.3 us (4%)
    ppermute x24, waiting for transfers between devices, swap_ctx(): return lax.ppermute(value, 'ctx', [(i, i ^ stride) for i in range(devices)])  55.7 us
    ppermute x24, starting transfers between devices, swap_ctx(): return lax.ppermute(value, 'ctx', [(i, i ^ stride) for i in range(devices)])  51.6 us
    all_gather x1, waiting for transfers between devices, body(): g_up_all = lax.all_gather(g_up_part, 'ctx', axis=0, tiled=True).astype(f32)  29.1 us
    dot_general x13, matrix products, mm(): return lax.dot_general(left, right, dims, preferred_element_type=f32)  27 us
    ppermute x14, waiting for transfers between devices, swap_x(): return lax.ppermute(value, 'fsdp', [(0, 1), (1, 0)])  17.7 us
    unnamed x5, waiting for transfers between devices  16.8 us
    ppermute x14, starting transfers between devices, swap_x(): return lax.ppermute(value, 'fsdp', [(0, 1), (1, 0)])  15.7 us
    select_n x15, other arithmetic, in_order(): jnp.where(bit == 0, jnp.concatenate([mine, theirs], axis=axis), jnp.conca...  12.7 us
  transfers between devices with their start and end apart: 42, of which 19 were waited for; matrix products, arithmetic and copies ran while one was open for 29% of the time, Pallas kernels for 4%

profile of v1, /device:TPU:0, one launch (start us, length us, event | category | flops | bytes accessed | tf_op | source)
XLA Modules:
  0.0 328.9 jit_solution(1674155806504132207)
XLA Ops:
  7.3 5.8 %concatenate.278 = bf16[4288]{0:T(1024)(128)(2,1)S(1)} concatenate(bf16[384]{0:T(512)(128)(2,1)} %param.24, bf16[384]{0:T(512)(128)(2,1)} %param.25, bf16[384]{0:T(512)(128)(2,1)} %param.26, bf16[384]{0:T(512)(128)(2,1)} %param.27, bf16[448]{0:T(512)(128)(2,1)} %param.29, bf16[384]{0:T(512)(128)(2,1)} %param.31, bf16[1536]{0:T(1024)(128)(2,1)} %param.33, bf16[384]{0:T(512)(128)(2,1)} %param.35), dimensions={0} | concatenate | bytes 17152 | tf_op jit(solution)/shard_map/concatenate | solution.py:313
  34.3 14.4 %collective-permute-done.8 = bf16[384,128]{1,0:T(8,128)(2,1)S(1)} collective-permute-done((bf16[384,128]{1,0:T(8,128)(2,1)S(1)}, bf16[384,128]{1,0:T(8,128)(2,1)S(1)}, u32[]{:S(2)}, u32[]{:S(2)}) %collective-permute-start.8) | collective-permute-done | bytes 98336 | tf_op jit(solution)/shard_map/ppermute | solution.py:42
  73.8 4.1 %collective-permute-done.3 = bf16[96,1536]{1,0:T(8,128)(2,1)S(1)} collective-permute-done((bf16[96,1536]{1,0:T(8,128)(2,1)}, bf16[96,1536]{1,0:T(8,128)(2,1)S(1)}, u32[]{:S(2)}, u32[]{:S(2)}) %collective-permute-start.3) | collective-permute-done | bytes 294944 | tf_op jit(solution)/shard_map/ppermute | solution.py:46
  83.8 3.1 multiply_convert_fusion
  88.0 3.8 %convolution_convert_fusion = bf16[1536,768]{1,0:T(8,128)(2,1)} fusion(bf16[512,1536]{1,0:T(8,128)(2,1)S(1)} %get-tuple-element.70, bf16[256,768]{1,0:T(8,128)(2,1)} %collective-permute-done.13, bf16[256,768]{1,0:T(8,128)(2,1)S(1)} %bitcast.76), kind=kOutput, calls=%fused_computation.1 | convolution fusion | flops 1210712064 | bytes 4718592 | tf_op jit(solution)/shard_map/dot_general | solution.py:21
  94.4 3.1 q.1.q_ref
  102.3 9.0 %attn.1 = (bf16[256,768]{1,0:T(8,128)(2,1)}, bf16[256,768]{1,0:T(8,128)(2,1)}, bf16[4096,128]{1,0:T(8,128)(2,1)}) custom-call(s32[1]{0:T(128)} %bitcast.5.ids_ref, s32[1,16]{1,0:T(1,128)} %len_ref.1, bf16[256,768]{1,0:T(8,128)(2,1)} %q.1.q_ref, bf16[4096,128]{1,0:T(8,128)(2,1)} %maximum_select_fusion.4.kv_ref, bf16[256,768]{1,0:T(8,128)(2,1)} %maximum_select_fusion.11.g_ref, ...), custom_call_target="tpu_custom_call" | custom-call | flops 20000000000 | bytes 4000000 | tf_op jit(solution)/shard_map/attn/pallas_call | solution.py:217
  111.4 4.4 %convert_reduce_fusion = (f32[1536]{0:T(1024)}, bf16[512,1536]{1,0:T(8,128)(2,1)S(1)}) fusion(f32[512,1536]{1,0:T(8,128)} %get-tuple-element.71, bf16[1536,768]{1,0:T(8,128)(2,1)S(1)} %copy-done, bf16[256,768]{1,0:T(8,128)(2,1)} %collective-permute-done.13, bf16[256,768]{1,0:T(8,128)(2,1)S(1)} %bitcast.77), kind=kOutput, calls=%fused_computation.9 | convolution fusion | flops 1218968064 | bytes 7870464 | tf_op jit(solution)/shard_map/dot_general | solution.py:21
  128.1 3.0 fusion.42
  141.0 4.3 %collective-permute-start.18 = (bf16[1024,128]{1,0:T(8,128)(2,1)S(1)}, bf16[1024,128]{1,0:T(8,128)(2,1)S(1)}, u32[]{:S(2)}, u32[]{:S(2)}) collective-permute-start(bf16[1024,128]{1,0:T(8,128)(2,1)S(1)} %dynamic-slice_convert_fusion.1), channel_id=1, source_target_pairs={{0,4},{2,6},{4,0},{6,2},{8,12},{10,14},{12,8},{14,10},{16,20},{18,... | collective-permute-start | bytes 786440 | tf_op jit(solution)/shard_map/ppermute | solution.py:46
  145.9 5.7 %collective-permute-done.18 = bf16[1024,128]{1,0:T(8,128)(2,1)S(1)} collective-permute-done((bf16[1024,128]{1,0:T(8,128)(2,1)S(1)}, bf16[1024,128]{1,0:T(8,128)(2,1)S(1)}, u32[]{:S(2)}, u32[]{:S(2)}) %collective-permute-start.18) | collective-permute-done | bytes 262176 | tf_op jit(solution)/shard_map/ppermute | solution.py:46
  159.5 23.8 %collective-permute-start.20 = (bf16[256,128]{1,0:T(8,128)(2,1)S(1)}, bf16[256,128]{1,0:T(8,128)(2,1)S(1)}, u32[]{:S(2)}, u32[]{:S(2)}) collective-permute-start(bf16[256,128]{1,0:T(8,128)(2,1)S(1)} %dynamic-slice_convert_fusion.5), channel_id=1, source_target_pairs={{0,16},{2,18},{4,20},{6,22},{8,24},{10,26},{12,28},{14,30},{16,0},... | collective-permute-start | bytes 196616 | tf_op jit(solution)/shard_map/ppermute | solution.py:46
  190.7 3.1 fusion.35
  200.9 3.9 %collective-permute-done.30 = bf16[96,1536]{1,0:T(8,128)(2,1)} collective-permute-done((bf16[96,1536]{1,0:T(8,128)(2,1)S(1)}, bf16[96,1536]{1,0:T(8,128)(2,1)}, u32[]{:S(2)}, u32[]{:S(2)}) %collective-permute-start.30) | collective-permute-done | bytes 294944 | tf_op jit(solution)/shard_map/ppermute | solution.py:46
  206.0 16.8 %reduce-scatter.7.cloned.1.call-done = bf16[24,3072]{1,0:T(8,128)(2,1)} async-done(((bf16[384,3072]{1,0:T(8,128)(2,1)}), bf16[24,3072]{1,0:T(8,128)(2,1)}) %reduce-scatter.7.cloned.1.call-update) | async-done | bytes 147472
  235.1 7.1 %collective-permute-done.32 = bf16[24,1536]{1,0:T(8,128)(2,1)S(1)} collective-permute-done((bf16[24,1536]{1,0:T(8,128)(2,1)S(1)}, bf16[24,1536]{1,0:T(8,128)(2,1)S(1)}, u32[]{:S(2)}, u32[]{:S(2)}) %collective-permute-start.32) | collective-permute-done | bytes 73760 | tf_op jit(solution)/shard_map/ppermute | solution.py:46
  242.4 5.2 %collective-permute-done.33 = bf16[24,1536]{1,0:T(8,128)(2,1)S(1)} collective-permute-done((bf16[24,1536]{1,0:T(8,128)(2,1)S(1)}, bf16[24,1536]{1,0:T(8,128)(2,1)S(1)}, u32[]{:S(2)}, u32[]{:S(2)}) %collective-permute-start.33) | collective-permute-done | bytes 73760 | tf_op jit(solution)/shard_map/ppermute | solution.py:46
  249.8 3.2 collective-permute-done.34
  253.0 3.5 %collective-permute-start.35 = (bf16[96,1536]{1,0:T(8,128)(2,1)S(1)}, bf16[96,1536]{1,0:T(8,128)(2,1)S(1)}, u32[]{:S(2)}, u32[]{:S(2)}) collective-permute-start(bf16[96,1536]{1,0:T(8,128)(2,1)S(1)} %maximum_select_fusion.13), channel_id=1, source_target_pairs={{0,4},{2,6},{4,0},{6,2},{8,12},{10,14},{12,8},{14,10},{16,20},{18,... | collective-permute-start | bytes 884744 | tf_op jit(solution)/shard_map/ppermute | solution.py:46
  260.3 11.1 %collective-permute-done.27 = f32[416,128]{1,0:T(8,128)S(1)} collective-permute-done((f32[416,128]{1,0:T(8,128)S(1)}, f32[416,128]{1,0:T(8,128)S(1)}, u32[]{:S(2)}, u32[]{:S(2)}) %collective-permute-start.27) | collective-permute-done | bytes 213024 | tf_op jit(solution)/shard_map/ppermute | solution.py:46
  274.6 4.9 %collective-permute-done.28 = f32[416,128]{1,0:T(8,128)S(1)} collective-permute-done((f32[416,128]{1,0:T(8,128)S(1)}, f32[416,128]{1,0:T(8,128)S(1)}, u32[]{:S(2)}, u32[]{:S(2)}) %collective-permute-start.28) | collective-permute-done | bytes 213024 | tf_op jit(solution)/shard_map/ppermute | solution.py:46
  284.1 4.2 %convert_element_type.233 = f32[1536,768]{1,0:T(8,128)} convert(bf16[1536,768]{1,0:T(8,128)(2,1)} %all-gather.5.cloned.1.call-done) | non-fusion elementwise | flops 1179648 | bytes 7077888 | tf_op jit(solution)/shard_map/convert_element_type | solution.py:380
  288.3 29.1 %all-gather.3.cloned.1.call-done = bf16[384,3072]{1,0:T(8,128)(2,1)} async-done(((bf16[24,3072]{1,0:T(8,128)(2,1)}), bf16[384,3072]{1,0:T(8,128)(2,1)}) %all-gather.3.cloned.1.call-update) | async-done | bytes 2359312 | tf_op jit(solution)/shard_map/all_gather | solution.py:381
  317.4 4.4 %convert_element_type.231 = f32[384,3072]{1,0:T(8,128)} convert(bf16[384,3072]{1,0:T(8,128)(2,1)} %all-gather.3.cloned.1.call-done) | non-fusion elementwise | flops 1179648 | bytes 7077888 | tf_op jit(solution)/shard_map/convert_element_type | solution.py:381
  (361 shorter events, 132.7 us)
Async XLA Ops:
  7.2 148.9 %reduce-scatter.5.cloned.1.call-start = ((), (), s32[]{:S(2)}) async-start(), calls=%async_computation.3 | async-start | bytes 2506752 | tf_op jit(solution)/shard_map/reduce_scatter | solution.py:375
  13.1 17.8 %collective-permute-start = (bf16[40,128]{1,0:T(8,128)(2,1)S(1)}, bf16[40,128]{1,0:T(8,128)(2,1)S(1)}, u32[]{:S(2)}, u32[]{:S(2)}) collective-permute-start(bf16[40,128]{1,0:T(8,128)(2,1)S(1)} %pad_bitcast_fusion.1), channel_id=1, source_target_pairs={{0,1},{1,0},{2,3},{3,2},{4,5},{5,4},{6,7},{7,6},{8,9},{9,8},{10,11... | collective-permute-start | bytes 30728 | tf_op jit(solution)/shard_map/ppermute | solution.py:42
  17.9 50.3 %collective-permute-start.2 = (bf16[96,1536]{1,0:T(8,128)(2,1)}, bf16[96,1536]{1,0:T(8,128)(2,1)}, u32[]{:S(2)}, u32[]{:S(2)}) collective-permute-start(bf16[96,1536]{1,0:T(8,128)(2,1)} %dynamic_slice.91), channel_id=1, source_target_pairs={{0,1},{1,0},{2,3},{3,2},{4,5},{5,4},{6,7},{7,6},{8,9},{9,8},{10,11... | collective-permute-start | bytes 884744 | tf_op jit(solution)/shard_map/ppermute | solution.py:42
  18.0 52.1 %collective-permute-start.1 = (bf16[256,768]{1,0:T(8,128)(2,1)}, bf16[256,768]{1,0:T(8,128)(2,1)S(1)}, u32[]{:S(2)}, u32[]{:S(2)}) collective-permute-start(bf16[256,768]{1,0:T(8,128)(2,1)} %bitcast.71), channel_id=1, source_target_pairs={{0,1},{1,0},{2,3},{3,2},{4,5},{5,4},{6,7},{7,6},{8,9},{9,8},{10,11... | collective-permute-start | bytes 1179656 | tf_op jit(solution)/shard_map/ppermute | solution.py:42
  19.9 50.3 %collective-permute-start.13 = (bf16[256,768]{1,0:T(8,128)(2,1)}, bf16[256,768]{1,0:T(8,128)(2,1)}, u32[]{:S(2)}, u32[]{:S(2)}) collective-permute-start(bf16[256,768]{1,0:T(8,128)(2,1)} %bitcast.73), channel_id=1, source_target_pairs={{0,1},{1,0},{2,3},{3,2},{4,5},{5,4},{6,7},{7,6},{8,9},{9,8},{10,11... | collective-permute-start | bytes 1179656 | tf_op jit(solution)/shard_map/ppermute | solution.py:42
  22.6 37.8 %collective-permute-start.5 = (bf16[96,768]{1,0:T(8,128)(2,1)}, bf16[96,768]{1,0:T(8,128)(2,1)}, u32[]{:S(2)}, u32[]{:S(2)}) collective-permute-start(bf16[96,768]{1,0:T(8,128)(2,1)} %constant_dynamic-slice_fusion.8), channel_id=1, source_target_pairs={{0,1},{1,0},{2,3},{3,2},{4,5},{5,4},{6,7},{7,6},{8,9},{9,8},{10,11... | collective-permute-start | bytes 442376 | tf_op jit(solution)/shard_map/ppermute | solution.py:42
  30.9 17.8 %collective-permute-start.8 = (bf16[384,128]{1,0:T(8,128)(2,1)S(1)}, bf16[384,128]{1,0:T(8,128)(2,1)S(1)}, u32[]{:S(2)}, u32[]{:S(2)}) collective-permute-start(bf16[384,128]{1,0:T(8,128)(2,1)S(1)} %slice.142), channel_id=1, source_target_pairs={{0,1},{1,0},{2,3},{3,2},{4,5},{5,4},{6,7},{7,6},{8,9},{9,8},{10,11... | collective-permute-start | bytes 294920 | tf_op jit(solution)/shard_map/ppermute | solution.py:42
  65.0 16.5 %collective-permute-start.11 = (bf16[1024,128]{1,0:T(8,128)(2,1)S(1)}, bf16[1024,128]{1,0:T(8,128)(2,1)S(1)}, u32[]{:S(2)}, u32[]{:S(2)}) collective-permute-start(bf16[1024,128]{1,0:T(8,128)(2,1)S(1)} %maximum_select_fusion.14), channel_id=1, source_target_pairs={{0,4},{2,6},{4,0},{6,2},{8,12},{10,14},{12,8},{14,10},{16,20},{18,... | collective-permute-start | bytes 786440 | tf_op jit(solution)/shard_map/ppermute | solution.py:46
  68.1 14.9 %collective-permute-start.7 = (bf16[192,768]{1,0:T(8,128)(2,1)S(1)}, bf16[192,768]{1,0:T(8,128)(2,1)S(1)}, u32[]{:S(2)}, u32[]{:S(2)}) collective-permute-start(bf16[192,768]{1,0:T(8,128)(2,1)S(1)} %maximum_select_fusion.12), channel_id=1, source_target_pairs={{0,2},{2,0},{4,6},{6,4},{8,10},{10,8},{12,14},{14,12},{16,18},{18,... | collective-permute-start | bytes 884744 | tf_op jit(solution)/shard_map/ppermute | solution.py:46
  73.0 24.5 %collective-permute-start.14 = (bf16[256,384]{1,0:T(8,128)(2,1)}, bf16[256,384]{1,0:T(8,128)(2,1)}, u32[]{:S(2)}, u32[]{:S(2)}) collective-permute-start(bf16[256,384]{1,0:T(8,128)(2,1)} %get-tuple-element.45), channel_id=1, source_target_pairs={{0,1},{1,0},{2,3},{3,2},{4,5},{5,4},{6,7},{7,6},{8,9},{9,8},{10,11... | collective-permute-start | bytes 589832 | tf_op jit(solution)/shard_map/ppermute | solution.py:42
  82.5 16.9 %collective-permute-start.12 = (bf16[2048,128]{1,0:T(8,128)(2,1)}, bf16[2048,128]{1,0:T(8,128)(2,1)}, u32[]{:S(2)}, u32[]{:S(2)}) collective-permute-start(bf16[2048,128]{1,0:T(8,128)(2,1)} %maximum_select_fusion.8), channel_id=1, source_target_pairs={{0,2},{2,0},{4,6},{6,4},{8,10},{10,8},{12,14},{14,12},{16,18},{18,... | collective-permute-start | bytes 1572872 | tf_op jit(solution)/shard_map/ppermute | solution.py:46
  91.9 130.9 %reduce-scatter.7.cloned.1.call-start = ((), (), s32[]{:S(2)}) async-start(), calls=%async_computation.5 | async-start | bytes 2506752
  121.5 162.6 %all-gather.5.cloned.1.call-start = ((), (), s32[]{:S(2)}) async-start(), calls=%async_computation.4 | async-start | bytes 2506752 | tf_op jit(solution)/shard_map/all_gather | solution.py:380
  123.0 17.9 %collective-permute-start.17 = (bf16[2048,128]{1,0:T(8,128)(2,1)S(1)}, bf16[2048,128]{1,0:T(8,128)(2,1)S(1)}, u32[]{:S(2)}, u32[]{:S(2)}) collective-permute-start(bf16[2048,128]{1,0:T(8,128)(2,1)S(1)} %constant_dynamic-slice_fusion.5), channel_id=1, source_target_pairs={{0,2},{2,0},{4,6},{6,4},{8,10},{10,8},{12,14},{14,12},{16,18},{18,... | collective-permute-start | bytes 1572872 | tf_op jit(solution)/shard_map/ppermute | solution.py:46
  125.2 15.6 %collective-permute-start.24 = (bf16[256,768]{1,0:T(8,128)(2,1)S(1)}, bf16[256,768]{1,0:T(8,128)(2,1)S(1)}, u32[]{:S(2)}, u32[]{:S(2)}) collective-permute-start(bf16[256,768]{1,0:T(8,128)(2,1)S(1)} %copy-done.15), channel_id=1, source_target_pairs={{0,1},{1,0},{2,3},{3,2},{4,5},{5,4},{6,7},{7,6},{8,9},{9,8},{10,11... | collective-permute-start | bytes 1179656 | tf_op jit(solution)/shard_map/ppermute | solution.py:42
  133.3 57.3 %collective-permute-start.21 = (bf16[256,768]{1,0:T(8,128)(2,1)}, bf16[256,768]{1,0:T(8,128)(2,1)}, u32[]{:S(2)}, u32[]{:S(2)}) collective-permute-start(bf16[256,768]{1,0:T(8,128)(2,1)} %slice.242), channel_id=1, source_target_pairs={{0,1},{1,0},{2,3},{3,2},{4,5},{5,4},{6,7},{7,6},{8,9},{9,8},{10,11... | collective-permute-start | bytes 1179656 | tf_op jit(solution)/shard_map/ppermute | solution.py:42
  135.4 136.4 %collective-permute-start.16 = (bf16[256,768]{1,0:T(8,128)(2,1)}, bf16[256,768]{1,0:T(8,128)(2,1)}, u32[]{:S(2)}, u32[]{:S(2)}) collective-permute-start(bf16[256,768]{1,0:T(8,128)(2,1)} %slice.243), channel_id=1, source_target_pairs={{0,1},{1,0},{2,3},{3,2},{4,5},{5,4},{6,7},{7,6},{8,9},{9,8},{10,11... | collective-permute-start | bytes 1179656 | tf_op jit(solution)/shard_map/ppermute | solution.py:42
  141.0 10.5 %collective-permute-start.18 = (bf16[1024,128]{1,0:T(8,128)(2,1)S(1)}, bf16[1024,128]{1,0:T(8,128)(2,1)S(1)}, u32[]{:S(2)}, u32[]{:S(2)}) collective-permute-start(bf16[1024,128]{1,0:T(8,128)(2,1)S(1)} %dynamic-slice_convert_fusion.1), channel_id=1, source_target_pairs={{0,4},{2,6},{4,0},{6,2},{8,12},{10,14},{12,8},{14,10},{16,20},{18,... | collective-permute-start | bytes 786440 | tf_op jit(solution)/shard_map/ppermute | solution.py:46
  156.1 161.3 %all-gather.3.cloned.1.call-start = ((), (), s32[]{:S(2)}) async-start(), calls=%async_computation.2 | async-start | bytes 2506752 | tf_op jit(solution)/shard_map/all_gather | solution.py:381
  159.5 26.2 %collective-permute-start.20 = (bf16[256,128]{1,0:T(8,128)(2,1)S(1)}, bf16[256,128]{1,0:T(8,128)(2,1)S(1)}, u32[]{:S(2)}, u32[]{:S(2)}) collective-permute-start(bf16[256,128]{1,0:T(8,128)(2,1)S(1)} %dynamic-slice_convert_fusion.5), channel_id=1, source_target_pairs={{0,16},{2,18},{4,20},{6,22},{8,24},{10,26},{12,28},{14,30},{16,0},... | collective-permute-start | bytes 196616 | tf_op jit(solution)/shard_map/ppermute | solution.py:46
  184.6 10.0 %collective-permute-start.29 = (bf16[192,1536]{1,0:T(8,128)(2,1)}, bf16[192,1536]{1,0:T(8,128)(2,1)S(1)}, u32[]{:S(2)}, u32[]{:S(2)}) collective-permute-start(bf16[192,1536]{1,0:T(8,128)(2,1)} %fusion.6), channel_id=1, source_target_pairs={{0,2},{2,0},{4,6},{6,4},{8,10},{10,8},{12,14},{14,12},{16,18},{18,... | collective-permute-start | bytes 1769480 | tf_op jit(solution)/shard_map/ppermute | solution.py:46
  247.9 10.9 %collective-permute-start.26 = (f32[416,128]{1,0:T(8,128)S(1)}, f32[416,128]{1,0:T(8,128)S(1)}, u32[]{:S(2)}, u32[]{:S(2)}) collective-permute-start(f32[416,128]{1,0:T(8,128)S(1)} %fusion.70), channel_id=1, source_target_pairs={{0,4},{2,6},{4,0},{6,2},{8,12},{10,14},{12,8},{14,10},{16,20},{18,... | collective-permute-start | bytes 638984 | tf_op jit(solution)/shard_map/ppermute | solution.py:46
  253.0 18.5 %collective-permute-start.35 = (bf16[96,1536]{1,0:T(8,128)(2,1)S(1)}, bf16[96,1536]{1,0:T(8,128)(2,1)S(1)}, u32[]{:S(2)}, u32[]{:S(2)}) collective-permute-start(bf16[96,1536]{1,0:T(8,128)(2,1)S(1)} %maximum_select_fusion.13), channel_id=1, source_target_pairs={{0,4},{2,6},{4,0},{6,2},{8,12},{10,14},{12,8},{14,10},{16,20},{18,... | collective-permute-start | bytes 884744 | tf_op jit(solution)/shard_map/ppermute | solution.py:46
  258.9 12.5 %collective-permute-start.27 = (f32[416,128]{1,0:T(8,128)S(1)}, f32[416,128]{1,0:T(8,128)S(1)}, u32[]{:S(2)}, u32[]{:S(2)}) collective-permute-start(f32[416,128]{1,0:T(8,128)S(1)} %add.382), channel_id=1, source_target_pairs={{0,8},{2,10},{4,12},{6,14},{8,0},{10,2},{12,4},{14,6},{16,24},{18,... | collective-permute-start | bytes 638984 | tf_op jit(solution)/shard_map/ppermute | solution.py:46
  (96 other events, 1578.6 us)
Sparse Core Ops, SparseCore 0:
  92.0 63.2 reduce-scatter.4
  160.1 62.7 reduce-scatter.6
  225.1 48.6 all-gather.4
  276.5 40.8 all-gather.2
